TPU v7x, 128 devices: a whole 4x4x4 slice. The times are simulated.
128 devices in a mesh: vae: 8 (over x_hi, z), seq: 16 (over x_lo, y, core).
Axes of the slice: x: 4 (x_hi: 2, x_lo: 2; x = x_hi * 2 + x_lo), y: 4, z: 4, core: 2. Of those that a mesh axis runs over, the one named last changes fastest.
Arguments:
- video: float32 [32, 256, 512], P('vae', 'seq')
- frame_counts: int32 [8], replicated, may hold values from 2 to 4, as said below
- conv_weight: float32 [3, 512, 512], replicated, may hold values from -0.15625 to 0.15625
- conv_bias: float32 [512], replicated, may hold values from -4 to 4
- norm_gain: float32 [512], replicated, may hold values from 0.1 to 1.9
- norm_bias: float32 [512], replicated, may hold values from -3 to 3
- embed_weight: bfloat16 [512, 3072], replicated, may hold values from -0.25 to 0.25
- embed_bias: float32 [3072], replicated, may hold values from -3 to 3
- shift: float32 [3072], replicated, may hold values from -3 to 3
- scale: float32 [3072], replicated, may hold values from -3 to 3
- gate: float32 [3072], replicated, may hold values from 1 to 3
- qkv_weight: bfloat16 [3072, 3, 3072], P(None, None, 'vae')
- q_gain: float32 [128], replicated, may hold values from 1 to 6
- k_gain: float32 [128], replicated, may hold values from 1 to 6
- out_weight: bfloat16 [3072, 3072], P('vae'), may hold values from -0.109375 to 0.109375
Outputs:
- result: bfloat16 [32, 256, 3072], P(None, 'seq', 'vae')
Inputs may be any that keep to these rules, and one draw needn't show every extreme that they name: `frame_counts`: every index of vae has at least 2 live slots; at least one has all 4 live.
All inputs are finite; a program needn't handle non-finite values.
Results may differ from a plain program's by a relative error of at most 0.013.
The roundings to bfloat16 on the way count: a program that leaves them out, or rounds other values in their place, can miss the bound.
Values may be sent and summed in bfloat16 or wider, within the bound.
A program may use at most 192 MiB of HBM per device.

v0:
```python
import math
import jax
import jax.numpy as jnp
from jax import lax
from jax.sharding import PartitionSpec as P

GROUPS = 32
HD = 128


def from_behind(x, axis, by):
    count = lax.axis_size(axis)
    pairs = [(i, i + by) for i in range(count) if 0 <= i + by < count]
    return lax.ppermute(x, axis, pairs)


def head_norm(values, weights):
    return values * lax.rsqrt(jnp.mean(values * values, axis=-1, keepdims=True) + 1e-06) * weights


def body(
    video,
    frame_counts,
    conv_weight,
    conv_bias,
    norm_gain,
    norm_bias,
    embed_weight,
    embed_bias,
    shift,
    scale,
    gate,
    qkv_weight,
    q_gain,
    k_gain,
    out_weight,
):
    highest = lax.Precision.HIGHEST
    fdev, pdev, chans = video.shape
    nvae = lax.axis_size("vae")
    nseq = lax.axis_size("seq")
    me_vae = lax.axis_index("vae")
    mine = frame_counts[me_vae]
    tail = lax.dynamic_slice_in_dim(video, mine - 2, 2, 0)
    prior = from_behind(tail, "vae", 1)
    extended = jnp.concatenate([prior, video], 0)
    conv = conv_bias + jnp.zeros((fdev, pdev, chans), jnp.float32)
    for tap in range(3):
        conv = conv + jnp.einsum(
            "fpc,cd->fpd", extended[2 - tap : 2 - tap + fdev], conv_weight[tap], precision=highest
        )
    local_live = (jnp.arange(fdev) < mine).astype(jnp.float32)[:, None, None]
    masked = conv * local_live
    width = chans // GROUPS
    first = masked.reshape(fdev, pdev, GROUPS, width).sum((0, 1, 3))
    second = (masked * conv).reshape(fdev, pdev, GROUPS, width).sum((0, 1, 3))
    first, second = lax.psum((first, second), ("vae", "seq"))
    number = jnp.sum(frame_counts).astype(jnp.float32) * (pdev * nseq * width)
    mean = first / number
    var = second / number - mean * mean
    centre = jnp.repeat(mean, width)
    inverse = jnp.repeat(lax.rsqrt(var + 1e-06), width)
    act = jax.nn.silu((conv - centre) * inverse * norm_gain + norm_bias).astype(jnp.bfloat16)
    frames_total = fdev * nvae
    slot_live = (jnp.arange(frames_total) % fdev < jnp.repeat(frame_counts, fdev)).astype(
        jnp.float32
    )
    count_frames = act.shape[0]
    projected = (
        jnp.dot(act.reshape(-1, chans), embed_weight, preferred_element_type=jnp.float32)
        + embed_bias
    )
    alive = lax.dynamic_slice_in_dim(slot_live, me_vae * fdev, count_frames, 0)
    own_tokens = (projected.reshape(count_frames, pdev, -1) * alive[:, None, None]).astype(
        jnp.bfloat16
    )
    tokens = lax.all_gather(own_tokens, "vae", axis=0, tiled=True)
    nloc = frames_total * pdev
    dwidth = tokens.shape[2]
    rows = tokens.reshape(nloc, dwidth).astype(jnp.float32)
    centred = rows - jnp.mean(rows, axis=-1, keepdims=True)
    spread = jnp.mean(centred * centred, axis=-1, keepdims=True)
    hidden = (centred * lax.rsqrt(spread + 1e-06) * (1.0 + scale) + shift).astype(jnp.bfloat16)
    proj = jnp.dot(hidden, qkv_weight.reshape(dwidth, -1), preferred_element_type=jnp.float32)
    inner = qkv_weight.shape[2]
    heads = inner // HD
    queries = head_norm(proj[:, :inner].reshape(nloc, heads, HD), q_gain).astype(jnp.bfloat16)
    keys = head_norm(proj[:, inner : 2 * inner].reshape(nloc, heads, HD), k_gain).astype(
        jnp.bfloat16
    )
    values = proj[:, 2 * inner :].reshape(nloc, heads, HD).astype(jnp.bfloat16)
    key_live = jnp.repeat(slot_live, pdev)
    root = math.sqrt(HD)
    best = jnp.full((heads, nloc), -1e30, jnp.float32)
    key_piece = lax.all_gather(keys, "seq", axis=0, tiled=True)
    value_piece = lax.all_gather(values, "seq", axis=0, tiled=True)
    length = key_piece.shape[0]
    alive = jnp.take(key_live, jnp.arange(length) % nloc) > 0.5
    scores = (
        jnp.einsum("nhd,khd->hnk", queries, key_piece, preferred_element_type=jnp.float32) / root
    )
    scores = jnp.where(alive[None, None, :], scores, -1e30)
    top = jnp.maximum(best, jnp.max(scores, axis=-1))
    weights = jnp.where(alive[None, None, :], jnp.exp(scores - top[..., None]), 0.0)
    summed = jnp.sum(weights, axis=-1)
    accum = jnp.einsum(
        "hnk,khd->nhd",
        weights.astype(jnp.bfloat16),
        value_piece,
        preferred_element_type=jnp.float32,
    )
    best, summed, accum = (top, summed, accum)
    attended = accum / jnp.transpose(summed, (1, 0))[..., None]
    merged = attended.reshape(nloc, inner).astype(jnp.bfloat16)
    partial_out = jnp.dot(merged, out_weight, preferred_element_type=jnp.float32)
    mixed = lax.psum_scatter(partial_out, "vae", scatter_dimension=1, tiled=True)
    columns = mixed.shape[1]
    residual = lax.dynamic_slice_in_dim(rows, me_vae * columns, columns, 1)
    gate_part = lax.dynamic_slice_in_dim(gate, me_vae * columns, columns, 0)
    result = ((residual + gate_part * mixed) * key_live[:, None]).astype(jnp.bfloat16)
    return result.reshape(frames_total, pdev, columns)


def solution(mesh):
    in_specs = (
        P("vae", "seq", None),
        P(),
        P(),
        P(),
        P(),
        P(),
        P(),
        P(),
        P(),
        P(),
        P(),
        P(None, None, "vae"),
        P(),
        P(),
        P("vae", None),
    )
    out_specs = P(None, "seq", "vae")
    return jax.shard_map(body, mesh=mesh, in_specs=in_specs, out_specs=out_specs, check_vma=False)
```

profile of v0, /device:TPU:0, one launch (start us, length us, event | category | flops | bytes accessed | tf_op | source)
XLA Modules:
  0.0 400.2 jit_solution(12064693817004700212)
XLA Ops:
  6.5 1.4 dynamic_slice.15
  10.1 3.9 collective-permute-start
  14.0 1.4 reduce_sum.89
  16.9 2.0 convolution_add_fusion.1
  20.5 2.0 fusion.10
  22.5 2.0 fusion.22
  24.9 65.9 %all-reduce = (f32[32]{0:T(128)S(1)}, f32[32]{0:T(128)S(1)}) all-reduce(f32[32]{0:T(128)S(1)} %reduce_sum.88, f32[32]{0:T(128)S(1)} %reduce_sum.92), channel_id=1, replica_groups=mesh['vae'=8,'seq'=16] {'vae','seq'}, use_global_device_ids=true, to_apply=%region_2.0 | all-reduce | flops 64 | bytes 512 | tf_op jit(solution)/shard_map/psum | solution.py:57
  91.9 1.4 convolution_add_fusion
  94.2 10.3 %copy.25 = bf16[3072,3,384]{0,2,1:T(8,128)(2,1)} copy(bf16[3072,3,384]{2,0,1:T(8,128)(2,1)} %param.26) | data formatting | bytes 14155776 | tf_op args[11]
  104.6 49.5 %all-gather.4.cloned.1.call-done = bf16[32,16,3072]{2,1,0:T(8,128)(2,1)} async-done(((bf16[4,16,3072]{2,1,0:T(8,128)(2,1)}), bf16[32,16,3072]{2,1,0:T(8,128)(2,1)}) %all-gather.4.cloned.1.call-update) | async-done | bytes 3145744 | tf_op jit(solution)/shard_map/all_gather | solution.py:77
  154.0 2.5 convert_reduce_fusion
  156.6 3.6 multiply_reduce_fusion
  160.2 1.7 add_convert_fusion
  161.9 4.3 %fusion.33 = f32[512,1152]{1,0:T(8,128)S(1)} fusion(bf16[512,3072]{1,0:T(8,128)(2,1)S(1)} %bitcast.49, bf16[3072,1152]{0,1:T(8,128)(2,1)S(1)} %bitcast.46), kind=kOutput, calls=%fused_computation.71 | convolution fusion | flops 3623878656 | bytes 12582912 | tf_op jit(solution)/shard_map/dot_general | solution.py:84
  166.3 1.3 copy-done.5
  169.4 1.2 slice.51
  172.0 51.2 %gather_fusion = f32[8192]{0:T(1024)S(1)} fusion(f32[512]{0:T(512)S(1)} %reshape.176, s32[8192]{0:T(1024)S(1)} %broadcast_clamp_fusion), kind=kCustom, calls=%fused_computation | custom fusion | bytes 98304 | tf_op jit(solution)/shard_map/jit(_take)/gather | solution.py:98
  223.6 21.7 %fusion = (f32[3,512]{1,0:T(4,128)S(1)}, f32[3,512,8192]{2,1,0:T(8,128)}) fusion(pred[8192]{0:T(1024)(128)(4,1)S(1)} %select_compare_fusion, bf16[8192,3,128]{2,0,1:T(8,128)(2,1)} %all-gather.8.cloned.1.call-done, f32[512,3,128]{0,2,1:T(8,128)S(1)} %bitcast.45, f32[128]{0:T(128)S(1)} %copy-done.6, f32[512,3]{0,1:T(4,128)S(1)} %add_rsqrt_fusion.2), kind=kOutput, calls=%fused_computation.3 | convolution fusion | flops 3259562496 | bytes 57430528 | tf_op jit(solution)/shard_map/nhd,khd->hnk/dot_general | solution.py:100
  245.3 23.2 %fusion.1 = f32[3,512]{1,0:T(4,128)S(1)} fusion(f32[3,512,8192]{2,1,0:T(8,128)} %get-tuple-element.15, f32[3,512]{1,0:T(4,128)S(1)} %broadcast_maximum_fusion, pred[8192]{0:T(1024)(128)(4,1)S(1)} %select_compare_fusion), kind=kLoop, calls=%fused_computation.4 | loop fusion | flops 62913024 | bytes 50352128 | tf_op jit(solution)/shard_map/reduce_sum | solution.py:105
  268.5 22.0 %divide_convert_fusion = bf16[512,3,128]{0,2,1:T(8,128)(2,1)S(1)} fusion(bf16[8192,3,128]{0,2,1:T(8,128)(2,1)} %all-gather.6.cloned.1.call-done, f32[3,512,8192]{2,1,0:T(8,128)} %get-tuple-element.15, f32[3,512]{1,0:T(4,128)S(1)} %broadcast_maximum_fusion, pred[8192]{0:T(1024)(128)(4,1)S(1)} %select_compare_fusion, f32[512,3]{0,1:T(4,128)S(1)} %bitcast.55), kind=kOutput, calls=%fused_computation.25 | convolution fusion | flops 3284533248 | bytes 57036800 | tf_op jit(solution)/shard_map/hnk,khd->nhd/dot_general | solution.py:106
  290.6 4.5 %fusion.34 = f32[512,3072]{1,0:T(8,128)} fusion(bf16[512,384]{0,1:T(8,128)(2,1)S(1)} %bitcast.52, bf16[384,3072]{1,0:T(8,128)(2,1)S(1)} %copy-done.4), kind=kOutput, calls=%fused_computation.72 | convolution fusion | flops 1207959552 | bytes 9043968 | tf_op jit(solution)/shard_map/dot_general | solution.py:115
  296.0 5.4 %bitcast_convert_fusion = f32[512,3072]{1,0:T(8,128)} fusion(bf16[32,16,3072]{2,1,0:T(8,128)(2,1)} %all-gather.4.cloned.1.call-done), kind=kLoop, calls=%fused_computation.70 | loop fusion | flops 1572864 | bytes 9437184 | tf_op jit(solution)/shard_map/convert_element_type | solution.py:80
  301.4 90.0 %reduce-scatter.2.cloned.1.call-done = f32[512,384]{1,0:T(8,128)} async-done(((f32[512,3072]{1,0:T(8,128)}), f32[512,384]{1,0:T(8,128)}) %reduce-scatter.2.cloned.1.call-update) | async-done | bytes 786448 | tf_op jit(solution)/shard_map/reduce_scatter | solution.py:116
  391.4 2.3 multiply_convert_fusion
  (69 shorter events, 10.3 us)
Async XLA Ops:
  6.5 85.4 %copy-start = (bf16[512,3072]{1,0:T(8,128)(2,1)S(1)}, bf16[512,3072]{1,0:T(8,128)(2,1)}, u32[]{:S(2)}) copy-start(bf16[512,3072]{1,0:T(8,128)(2,1)} %param.21) | copy-start | bytes 9437188
  6.5 147.5 %all-gather.4.cloned.1.call-start = ((), (), s32[]{:S(2)}) async-start(), calls=%async_computation.1 | async-start | bytes 3538944 | tf_op jit(solution)/shard_map/all_gather | solution.py:77
  10.1 9.5 %collective-permute-start = (f32[2,16,512]{2,1,0:T(8,128)S(1)}, f32[2,16,512]{2,1,0:T(8,128)S(1)}, u32[]{:S(2)}, u32[]{:S(2)}) collective-permute-start(f32[2,16,512]{2,1,0:T(8,128)S(1)} %constant_dynamic-slice_fusion), channel_id=1, source_target_pairs={{0,16},{16,32},{32,48},{48,64},{64,80},{80,96},{96,112},{1,17},{17... | collective-permute-start | bytes 196616 | tf_op jit(solution)/shard_map/ppermute | solution.py:14
  94.2 10.4 %copy-start.8 = (f32[3072]{0:T(1024)S(1)}, f32[3072]{0:T(1024)}, u32[]{:S(2)}) copy-start(f32[3072]{0:T(1024)} %param.24) | copy-start | bytes 36868
  94.2 129.4 %all-gather.8.cloned.1.call-start = ((), (), s32[]{:S(2)}) async-start(), calls=%async_computation.3 | async-start | bytes 6684672 | tf_op jit(solution)/shard_map/all_gather | solution.py:95
  104.5 55.6 %copy-start.7 = (f32[3072]{0:T(1024)S(1)}, f32[3072]{0:T(1024)}, u32[]{:S(2)}) copy-start(f32[3072]{0:T(1024)} %param.23) | copy-start | bytes 36868
  154.0 6.2 %copy-start.2 = (bf16[32,16,3072]{2,1,0:T(8,128)(2,1)S(1)}, bf16[32,16,3072]{2,1,0:T(8,128)(2,1)}, u32[]{:S(2)}) copy-start(bf16[32,16,3072]{2,1,0:T(8,128)(2,1)} %all-gather.4.cloned.1.call-done) | copy-start | bytes 9437188
  154.0 7.9 %copy-start.3 = (bf16[3072,3,384]{0,2,1:T(8,128)(2,1)S(1)}, bf16[3072,3,384]{0,2,1:T(8,128)(2,1)}, u32[]{:S(2)}) copy-start(bf16[3072,3,384]{0,2,1:T(8,128)(2,1)} %copy.25) | copy-start | bytes 21233668
  166.2 1.4 copy-start.5
  166.2 2.1 copy-start.9
  169.3 99.2 %all-gather.6.cloned.1.call-start = ((), (), s32[]{:S(2)}) async-start(), calls=%async_computation.2 | async-start | bytes 6684672 | tf_op jit(solution)/shard_map/all_gather | solution.py:96
  171.5 219.9 %reduce-scatter.2.cloned.1.call-start = ((), (), s32[]{:S(2)}) async-start(), calls=%async_computation.4 | async-start | bytes 7077888 | tf_op jit(solution)/shard_map/reduce_scatter | solution.py:116
  171.9 51.7 %copy-start.6 = (f32[128]{0:T(128)S(1)}, f32[128]{0:T(128)}, u32[]{:S(2)}) copy-start(f32[128]{0:T(128)} %param.27) | copy-start | bytes 1540
  268.5 22.0 %copy-start.4 = (bf16[384,3072]{1,0:T(8,128)(2,1)S(1)}, bf16[384,3072]{1,0:T(8,128)(2,1)}, u32[]{:S(2)}) copy-start(bf16[384,3072]{1,0:T(8,128)(2,1)} %param.29) | copy-start | bytes 7077892
  295.1 98.6 %copy-start.1 = (bf16[512,3072]{1,0:T(8,128)(2,1)S(1)}, bf16[512,3072]{1,0:T(8,128)(2,1)}, u32[]{:S(2)}) copy-start(bf16[512,3072]{1,0:T(8,128)(2,1)} %param.21) | copy-start | bytes 9437188
Sparse Core Ops, SparseCore 0:
  94.3 59.7 all-gather.3
  169.4 40.0 all-gather.7
  211.2 43.1 all-gather.5
  295.2 96.1 reduce-scatter.1
where the time goes:
time: 401 us; the launch traced here: 400 us
  waiting for transfers between devices  140 us (35%)
  local copies, waits for them, and re-layouts  71.5 us (18%)
  blocking collectives  65.9 us (16%)
  matrix products  59.8 us (15%)
  other arithmetic  43.8 us (11%)
  between operations  15.4 us (4%)
  starting transfers between devices  4.23 us (1%)
    reduce_scatter x1, waiting for transfers between devices, body(): lax.psum_scatter(partial_out, 'vae', scatter_dimension=1, tiled=True)  90 us
    psum x1, blocking collectives, body(): first, second = lax.psum((first, second), ('vae', 'seq'))  65.9 us
    gather x1, local copies, waits for them, and re-layouts, body(): alive = jnp.take(key_live, jnp.arange(length) % nloc) > 0.5  51.2 us
    all_gather x1, waiting for transfers between devices, body(): tokens = lax.all_gather(own_tokens, 'vae', axis=0, tiled=True)  49.5 us
    reduce_sum x1, other arithmetic, body(): summed = jnp.sum(weights, axis=-1)  23.2 us
    dot_general x1, matrix products, body(): jnp.einsum('hnk,khd->nhd', weights.astype(jnp.bfloat16), value_piece, pre...  22 us
    dot_general x1, matrix products, body(): jnp.einsum('nhd,khd->hnk', queries, key_piece, preferred_element_type=jnp...  21.7 us
    unnamed x22, local copies, waits for them, and re-layouts  11.7 us
  transfers between devices with their start and end apart: 5, of which 2 were waited for; matrix products, arithmetic and copies ran while one was open for 30% of the time, Pallas kernels for 0%

commit v1 on v0

--- a/solution.py
+++ b/solution.py
@@ -74,7 +74,9 @@
     own_tokens = (projected.reshape(count_frames, pdev, -1) * alive[:, None, None]).astype(
         jnp.bfloat16
     )
-    tokens = lax.all_gather(own_tokens, "vae", axis=0, tiled=True)
+    tokens = jnp.concatenate(
+        lax.all_to_all(jnp.stack([own_tokens] * lax.axis_size("vae")), "vae", 0, 0), axis=0
+    )
     nloc = frames_total * pdev
     dwidth = tokens.shape[2]
     rows = tokens.reshape(nloc, dwidth).astype(jnp.float32)

time: 401 us -> 381 us (0.950)
  waiting for transfers between devices: 140 us -> 117 us
  other arithmetic: 43.8 us -> 38.4 us
  starting transfers between devices: 4.23 us -> 8.89 us
    all_gather x1 -> x0, waiting for transfers between devices: 49.5 us -> none  [body(): tokens = lax.all_gather(own_tokens, 'vae', axis=0, tiled=True)]
    all_to_all x0 -> x1, waiting for transfers between devices: none -> 27.2 us  [body(): lax.all_to_all(jnp.stack([own_tokens] * lax.axis_size('vae')), 'vae', 0, 0)]
    all_to_all x0 -> x1, starting transfers between devices: none -> 4.45 us  [body(): lax.all_to_all(jnp.stack([own_tokens] * lax.axis_size('vae')), 'vae', 0, 0)]
  transfers between devices with their start and end apart: 5 -> 5, of which waited for: 2 -> 2; matrix products, arithmetic and copies ran while one was open for 30% -> 32% of each run, Pallas kernels for 0% -> 0%
where the time goes in v1:
time: 381 us; the launch traced here: 380 us
  waiting for transfers between devices  117 us (31%)
  local copies, waits for them, and re-layouts  74.4 us (20%)
  blocking collectives  65.9 us (17%)
  matrix products  59.8 us (16%)
  other arithmetic  38.4 us (10%)
  between operations  15.4 us (4%)
  starting transfers between devices  8.89 us (2%)
    reduce_scatter x1, waiting for transfers between devices, body(): lax.psum_scatter(partial_out, 'vae', scatter_dimension=1, tiled=True)  90.1 us
    psum x1, blocking collectives, body(): first, second = lax.psum((first, second), ('vae', 'seq'))  65.9 us
    gather x1, local copies, waits for them, and re-layouts, body(): alive = jnp.take(key_live, jnp.arange(length) % nloc) > 0.5  51.2 us
    all_to_all x1, waiting for transfers between devices, body(): lax.all_to_all(jnp.stack([own_tokens] * lax.axis_size('vae')), 'vae', 0, 0)  27.2 us
    reduce_sum x1, other arithmetic, body(): summed = jnp.sum(weights, axis=-1)  23.2 us
    dot_general x1, matrix products, body(): jnp.einsum('hnk,khd->nhd', weights.astype(jnp.bfloat16), value_piece, pre...  22 us
    dot_general x1, matrix products, body(): jnp.einsum('nhd,khd->hnk', queries, key_piece, preferred_element_type=jnp...  21.7 us
    unnamed x22, local copies, waits for them, and re-layouts  12.5 us
  transfers between devices with their start and end apart: 5, of which 2 were waited for; matrix products, arithmetic and copies ran while one was open for 32% of the time, Pallas kernels for 0%

profile of v1, /device:TPU:0, one launch (start us, length us, event | category | flops | bytes accessed | tf_op | source)
XLA Modules:
  0.0 380.2 jit_solution(11902690550081406978)
XLA Ops:
  6.5 1.4 dynamic_slice.15
  10.1 3.9 %collective-permute-start = (f32[2,16,512]{2,1,0:T(8,128)S(1)}, f32[2,16,512]{2,1,0:T(8,128)S(1)}, u32[]{:S(2)}, u32[]{:S(2)}) collective-permute-start(f32[2,16,512]{2,1,0:T(8,128)S(1)} %constant_dynamic-slice_fusion), channel_id=1, source_target_pairs={{0,16},{16,32},{32,48},{48,64},{64,80},{80,96},{96,112},{1,17},{17... | collective-permute-start | bytes 196616 | tf_op jit(solution)/shard_map/ppermute | solution.py:14
  14.0 1.4 reduce_sum.89
  16.9 2.0 convolution_add_fusion.1
  20.5 2.0 fusion.10
  22.5 2.0 fusion.22
  24.9 65.9 %all-reduce = (f32[32]{0:T(128)S(1)}, f32[32]{0:T(128)S(1)}) all-reduce(f32[32]{0:T(128)S(1)} %reduce_sum.88, f32[32]{0:T(128)S(1)} %reduce_sum.92), channel_id=1, replica_groups=mesh['vae'=8,'seq'=16] {'vae','seq'}, use_global_device_ids=true, to_apply=%region_2.0 | all-reduce | flops 64 | bytes 512 | tf_op jit(solution)/shard_map/psum | solution.py:57
  91.9 1.4 convolution_add_fusion
  93.4 2.1 stack.2
  95.5 4.4 %all-to-all-start = ((bf16[8,4,16,3072]{3,2,1,0:T(8,128)(2,1)}), bf16[8,4,16,3072]{3,2,1,0:T(8,128)(2,1)S(1)}, u32[]{:S(2)}, u32[]{:S(2)}) async-start(bf16[8,4,16,3072]{3,2,1,0:T(8,128)(2,1)} %stack.2), calls=%async_computation | async-start | bytes 6291456 | tf_op jit(solution)/shard_map/all_to_all | solution.py:78
  100.2 10.3 %copy.19 = bf16[3072,3,384]{0,2,1:T(8,128)(2,1)} copy(bf16[3072,3,384]{2,0,1:T(8,128)(2,1)} %param.26) | data formatting | bytes 14155776 | tf_op args[11]
  110.5 27.2 %all-to-all-done = bf16[8,4,16,3072]{3,2,1,0:T(8,128)(2,1)S(1)} async-done(((bf16[8,4,16,3072]{3,2,1,0:T(8,128)(2,1)}), bf16[8,4,16,3072]{3,2,1,0:T(8,128)(2,1)S(1)}, u32[]{:S(2)}, u32[]{:S(2)}) %all-to-all-start) | async-done | bytes 3145760 | tf_op jit(solution)/shard_map/all_to_all | solution.py:78
  139.1 1.7 add_convert_fusion
  141.8 4.3 %fusion.33 = f32[512,1152]{1,0:T(8,128)S(1)} fusion(bf16[512,3072]{1,0:T(8,128)(2,1)S(1)} %bitcast.49, bf16[3072,1152]{0,1:T(8,128)(2,1)S(1)} %bitcast.46), kind=kOutput, calls=%fused_computation.71 | convolution fusion | flops 3623878656 | bytes 12582912 | tf_op jit(solution)/shard_map/dot_general | solution.py:86
  146.2 1.3 copy-done.5
  149.2 1.2 slice.51
  151.8 51.2 %gather_fusion = f32[8192]{0:T(1024)S(1)} fusion(f32[512]{0:T(512)S(1)} %reshape.178, s32[8192]{0:T(1024)S(1)} %broadcast_clamp_fusion), kind=kCustom, calls=%fused_computation | custom fusion | bytes 98304 | tf_op jit(solution)/shard_map/jit(_take)/gather | solution.py:100
  203.5 21.7 %fusion = (f32[3,512]{1,0:T(4,128)S(1)}, f32[3,512,8192]{2,1,0:T(8,128)}) fusion(pred[8192]{0:T(1024)(128)(4,1)S(1)} %select_compare_fusion, bf16[8192,3,128]{2,0,1:T(8,128)(2,1)} %all-gather.5.cloned.1.call-done, f32[512,3,128]{0,2,1:T(8,128)S(1)} %bitcast.45, f32[128]{0:T(128)S(1)} %copy-done.6, f32[512,3]{0,1:T(4,128)S(1)} %add_rsqrt_fusion.2), kind=kOutput, calls=%fused_computation.3 | convolution fusion | flops 3259562496 | bytes 57430528 | tf_op jit(solution)/shard_map/nhd,khd->hnk/dot_general | solution.py:102
  225.2 23.2 %fusion.1 = f32[3,512]{1,0:T(4,128)S(1)} fusion(f32[3,512,8192]{2,1,0:T(8,128)} %get-tuple-element.15, f32[3,512]{1,0:T(4,128)S(1)} %broadcast_maximum_fusion, pred[8192]{0:T(1024)(128)(4,1)S(1)} %select_compare_fusion), kind=kLoop, calls=%fused_computation.4 | loop fusion | flops 62913024 | bytes 50352128 | tf_op jit(solution)/shard_map/reduce_sum | solution.py:107
  248.4 22.0 %divide_convert_fusion = bf16[512,3,128]{0,2,1:T(8,128)(2,1)S(1)} fusion(bf16[8192,3,128]{0,2,1:T(8,128)(2,1)} %all-gather.3.cloned.1.call-done, f32[3,512,8192]{2,1,0:T(8,128)} %get-tuple-element.15, f32[3,512]{1,0:T(4,128)S(1)} %broadcast_maximum_fusion, pred[8192]{0:T(1024)(128)(4,1)S(1)} %select_compare_fusion, f32[512,3]{0,1:T(4,128)S(1)} %bitcast.55), kind=kOutput, calls=%fused_computation.25 | convolution fusion | flops 3284533248 | bytes 57036800 | tf_op jit(solution)/shard_map/hnk,khd->nhd/dot_general | solution.py:108
  270.4 4.5 %fusion.34 = f32[512,3072]{1,0:T(8,128)} fusion(bf16[512,384]{0,1:T(8,128)(2,1)S(1)} %bitcast.52, bf16[384,3072]{1,0:T(8,128)(2,1)S(1)} %copy-done.4), kind=kOutput, calls=%fused_computation.72 | convolution fusion | flops 1207959552 | bytes 9043968 | tf_op jit(solution)/shard_map/dot_general | solution.py:117
  275.9 5.4 %bitcast_convert_fusion = f32[512,3072]{1,0:T(8,128)} fusion(bf16[8,4,16,3072]{3,2,1,0:T(8,128)(2,1)} %copy-done.2), kind=kLoop, calls=%fused_computation.70 | loop fusion | flops 1572864 | bytes 9437184 | tf_op jit(solution)/shard_map/convert_element_type | solution.py:82
  281.3 90.1 %reduce-scatter.2.cloned.1.call-done = f32[512,384]{1,0:T(8,128)} async-done(((f32[512,3072]{1,0:T(8,128)}), f32[512,384]{1,0:T(8,128)}) %reduce-scatter.2.cloned.1.call-update) | async-done | bytes 786448 | tf_op jit(solution)/shard_map/reduce_scatter | solution.py:118
  371.4 2.3 multiply_convert_fusion
  (69 shorter events, 12.1 us)
Async XLA Ops:
  6.5 85.4 %copy-start = (bf16[512,3072]{1,0:T(8,128)(2,1)S(1)}, bf16[512,3072]{1,0:T(8,128)(2,1)}, u32[]{:S(2)}) copy-start(bf16[512,3072]{1,0:T(8,128)(2,1)} %param.21) | copy-start | bytes 9437188
  10.1 9.5 %collective-permute-start = (f32[2,16,512]{2,1,0:T(8,128)S(1)}, f32[2,16,512]{2,1,0:T(8,128)S(1)}, u32[]{:S(2)}, u32[]{:S(2)}) collective-permute-start(f32[2,16,512]{2,1,0:T(8,128)S(1)} %constant_dynamic-slice_fusion), channel_id=1, source_target_pairs={{0,16},{16,32},{32,48},{48,64},{64,80},{80,96},{96,112},{1,17},{17... | collective-permute-start | bytes 196616 | tf_op jit(solution)/shard_map/ppermute | solution.py:14
  95.5 42.1 %all-to-all-start = ((bf16[8,4,16,3072]{3,2,1,0:T(8,128)(2,1)}), bf16[8,4,16,3072]{3,2,1,0:T(8,128)(2,1)S(1)}, u32[]{:S(2)}, u32[]{:S(2)}) async-start(bf16[8,4,16,3072]{3,2,1,0:T(8,128)(2,1)} %stack.2), calls=%async_computation | async-start | bytes 6291456 | tf_op jit(solution)/shard_map/all_to_all | solution.py:78
  99.9 10.5 %copy-start.8 = (f32[3072]{0:T(1024)S(1)}, f32[3072]{0:T(1024)}, u32[]{:S(2)}) copy-start(f32[3072]{0:T(1024)} %param.24) | copy-start | bytes 36868
  99.9 103.5 %all-gather.5.cloned.1.call-start = ((), (), s32[]{:S(2)}) async-start(), calls=%async_computation.3 | async-start | bytes 6684672 | tf_op jit(solution)/shard_map/all_gather | solution.py:97
  110.5 28.7 %copy-start.7 = (f32[3072]{0:T(1024)S(1)}, f32[3072]{0:T(1024)}, u32[]{:S(2)}) copy-start(f32[3072]{0:T(1024)} %param.23) | copy-start | bytes 36868
  137.6 3.2 copy-start.2
  137.6 4.1 %copy-start.3 = (bf16[3072,3,384]{0,2,1:T(8,128)(2,1)S(1)}, bf16[3072,3,384]{0,2,1:T(8,128)(2,1)}, u32[]{:S(2)}) copy-start(bf16[3072,3,384]{0,2,1:T(8,128)(2,1)} %copy.19) | copy-start | bytes 21233668
  146.0 1.4 copy-start.5
  146.0 2.1 copy-start.9
  149.1 99.2 %all-gather.3.cloned.1.call-start = ((), (), s32[]{:S(2)}) async-start(), calls=%async_computation.2 | async-start | bytes 6684672 | tf_op jit(solution)/shard_map/all_gather | solution.py:98
  151.3 220.1 %reduce-scatter.2.cloned.1.call-start = ((), (), s32[]{:S(2)}) async-start(), calls=%async_computation.4 | async-start | bytes 7077888 | tf_op jit(solution)/shard_map/reduce_scatter | solution.py:118
  151.8 51.7 %copy-start.6 = (f32[128]{0:T(128)S(1)}, f32[128]{0:T(128)}, u32[]{:S(2)}) copy-start(f32[128]{0:T(128)} %param.27) | copy-start | bytes 1540
  248.4 22.0 %copy-start.4 = (bf16[384,3072]{1,0:T(8,128)(2,1)S(1)}, bf16[384,3072]{1,0:T(8,128)(2,1)}, u32[]{:S(2)}) copy-start(bf16[384,3072]{1,0:T(8,128)(2,1)} %param.29) | copy-start | bytes 7077892
  275.0 98.7 %copy-start.1 = (bf16[512,3072]{1,0:T(8,128)(2,1)S(1)}, bf16[512,3072]{1,0:T(8,128)(2,1)}, u32[]{:S(2)}) copy-start(bf16[512,3072]{1,0:T(8,128)(2,1)} %param.21) | copy-start | bytes 9437188
Sparse Core Ops, SparseCore 0:
  149.3 40.1 all-gather.4
  191.1 43.1 all-gather.2
  275.1 96.2 reduce-scatter.1
